TPU v7x, 256 devices: a whole 4x4x8 slice. The times are simulated.
256 devices in a mesh: depth: 4 (over x), row: 16 (over z, y_hi), col: 4 (over y_lo, core).
Axes of the slice: x: 4, y: 4 (y_hi: 2, y_lo: 2; y = y_hi * 2 + y_lo), z: 8, core: 2. Of those that a mesh axis runs over, the one named last changes fastest.
Arguments:
- tokens: bfloat16 [768, 8192], P(('depth', 'row')), may hold values from -6 to 6
- out_grad: bfloat16 [768, 8192], P(('depth', 'row')), may hold values from -0.59765625 to 0.59765625
- gate_weight: bfloat16 [8192, 16384], P('depth', ('row', 'col')), may hold values from -0.0625 to 0.0625
- up_weight: bfloat16 [8192, 16384], P('depth', ('row', 'col')), may hold values from -0.0625 to 0.0625
- down_weight: bfloat16 [16384, 8192], P(('row', 'col'), 'depth'), may hold values from -0.046875 to 0.046875
Outputs:
- input_grad: bfloat16 [768, 8192], P(('depth', 'row', 'col'))
- gate_grad: bfloat16 [8192, 16384], P('depth', ('row', 'col'))
- up_grad: bfloat16 [8192, 16384], P('depth', ('row', 'col'))
- down_grad: bfloat16 [16384, 8192], P(('row', 'col'), 'depth')
All inputs are finite; a program needn't handle non-finite values.
Results may differ from a plain program's by a relative error of at most 0.024.
Values may be sent and summed in bfloat16 or wider, within the bound.
No kernel may reach another device: no remote copies, remote signals or barrier semaphores. Data moves between devices by JAX's collectives and lax.ppermute only.
A program may use at most 128 MiB of HBM per device.

v0:
```python
import jax
import jax.numpy as jnp
from jax import lax
from jax.sharding import PartitionSpec as P


def contract_rows(left, right):
    return lax.dot_general(
        left, right, (((0,), (0,)), ((), ())), preferred_element_type=jnp.float32
    )


def contract_cols(left, right):
    return lax.dot_general(
        left, right, (((1,), (1,)), ((), ())), preferred_element_type=jnp.float32
    )


def swiglu_terms(gate, up, hidden_grad):
    sig = jax.nn.sigmoid(gate)
    act = gate * sig
    hidden = (act * up).astype(jnp.bfloat16)
    gate_term = (hidden_grad * up * sig * (1.0 + gate * (1.0 - sig))).astype(jnp.bfloat16)
    up_term = (hidden_grad * act).astype(jnp.bfloat16)
    return (hidden, gate_term, up_term)


def block_work(tok_part, grad_part, gate_full, up_full, down_full):
    gate = jnp.dot(tok_part, gate_full, preferred_element_type=jnp.float32)
    up = jnp.dot(tok_part, up_full, preferred_element_type=jnp.float32)
    hidden_grad = contract_cols(grad_part, down_full)
    hidden, gate_term, up_term = swiglu_terms(gate, up, hidden_grad)
    partial_in = contract_cols(gate_term, gate_full) + contract_cols(up_term, up_full)
    return (hidden, gate_term, up_term, partial_in)


def on_device(tokens, out_grad, gate_weight, up_weight, down_weight):
    gate_full, up_full, down_full = (
        lax.all_gather(gate_weight, "depth", axis=0, tiled=True),
        lax.all_gather(up_weight, "depth", axis=0, tiled=True),
        lax.all_gather(down_weight, "depth", axis=1, tiled=True),
    )
    all_tok, all_grad = (
        lax.all_gather(tokens, "row", axis=0, tiled=True),
        lax.all_gather(out_grad, "row", axis=0, tiled=True),
    )
    hidden, gate_term, up_term, partial_in = block_work(
        all_tok, all_grad, gate_full, up_full, down_full
    )
    input_grad = lax.psum_scatter(
        partial_in, ("row", "col"), scatter_dimension=0, tiled=True
    ).astype(jnp.bfloat16)
    gate_grad, up_grad, down_grad = (
        lax.psum_scatter(
            contract_rows(all_tok, gate_term).astype(jnp.bfloat16),
            "depth",
            scatter_dimension=0,
            tiled=True,
        ).astype(jnp.float32),
        lax.psum_scatter(
            contract_rows(all_tok, up_term).astype(jnp.bfloat16),
            "depth",
            scatter_dimension=0,
            tiled=True,
        ).astype(jnp.float32),
        lax.psum_scatter(
            contract_rows(hidden, all_grad).astype(jnp.bfloat16),
            "depth",
            scatter_dimension=1,
            tiled=True,
        ).astype(jnp.float32),
    )
    return (
        input_grad,
        gate_grad.astype(jnp.bfloat16),
        up_grad.astype(jnp.bfloat16),
        down_grad.astype(jnp.bfloat16),
    )


def solution(mesh):
    return jax.shard_map(
        on_device,
        mesh=mesh,
        in_specs=(
            P(("depth", "row"), None),
            P(("depth", "row"), None),
            P("depth", ("row", "col")),
            P("depth", ("row", "col")),
            P(("row", "col"), "depth"),
        ),
        out_specs=(
            P(("depth", "row", "col"), None),
            P("depth", ("row", "col")),
            P("depth", ("row", "col")),
            P(("row", "col"), "depth"),
        ),
        check_vma=False,
    )
```

profile of v0, /device:TPU:2, one launch (start us, length us, event | category | flops | bytes accessed | tf_op | source)
XLA Modules:
  0.0 703.7 jit_solution(15544658315042769333)
XLA Ops:
  7.2 0.7 all-gather.16.cloned.1.call-update
  7.9 0.7 all-gather.14.cloned.1.call-update
  8.7 0.7 all-gather.10.cloned.1.call-update
  10.6 103.0 %all-gather.16.cloned.1.call-done = bf16[16,12,8192]{2,1,0:T(8,128)(2,1)} async-done(((bf16[1,12,8192]{2,1,0:T(8,128)(2,1)}), bf16[16,12,8192]{2,1,0:T(8,128)(2,1)}) %all-gather.16.cloned.1.call-update) | async-done | bytes 3145744 | tf_op jit(solution)/shard_map/all_gather | solution.py:44
  113.6 3.2 reshape.11
  116.9 95.9 %all-gather.14.cloned.1.call-done = bf16[16,12,8192]{2,1,0:T(8,128)(2,1)} async-done(((bf16[1,12,8192]{2,1,0:T(8,128)(2,1)}), bf16[16,12,8192]{2,1,0:T(8,128)(2,1)}) %all-gather.14.cloned.1.call-update) | async-done | bytes 3145744 | tf_op jit(solution)/shard_map/all_gather | solution.py:45
  212.7 4.7 reshape.9
  217.4 43.8 %all-gather.10.cloned.1.call-done = bf16[8192,256]{1,0:T(8,128)(2,1)} async-done(((bf16[2048,256]{1,0:T(8,128)(2,1)}), bf16[8192,256]{1,0:T(8,128)(2,1)}) %all-gather.10.cloned.1.call-update) | async-done | bytes 4194320 | tf_op jit(solution)/shard_map/all_gather | solution.py:40
  261.3 3.2 fusion.5
  264.4 49.7 %all-gather.12.cloned.1.call-done = bf16[8192,256]{1,0:T(8,128)(2,1)} async-done(((bf16[2048,256]{1,0:T(8,128)(2,1)}), bf16[8192,256]{1,0:T(8,128)(2,1)}) %all-gather.12.cloned.1.call-update) | async-done | bytes 4194320 | tf_op jit(solution)/shard_map/all_gather | solution.py:39
  314.1 3.2 fusion.6
  317.3 49.7 %all-gather.8.cloned.1.call-done = bf16[256,8192]{1,0:T(8,128)(2,1)} async-done(((bf16[256,2048]{1,0:T(8,128)(2,1)}), bf16[256,8192]{1,0:T(8,128)(2,1)}) %all-gather.8.cloned.1.call-update) | async-done | bytes 4194320 | tf_op jit(solution)/shard_map/all_gather | solution.py:41
  367.0 5.3 multiply_convert_fusion.1
  372.3 0.6 copy-done.3
  373.0 3.2 fusion.1
  376.2 4.2 fusion
  380.5 1.8 copy-done.1
  382.3 3.3 convolution_convert_fusion
  386.8 4.4 fusion.7
  391.2 4.2 convolution_add_fusion
  395.4 296.2 %all-reduce.2 = bf16[192,8192]{1,0:T(8,128)(2,1)S(1)} all-reduce(f32[192,8192]{1,0:T(8,128)} %convolution_add_fusion), channel_id=2, replica_groups=mesh['depth'=4,'row'=16,'col'=4] {'row','col'}, use_global_device_ids=true, to_apply=%region_0.0.clone | all-reduce | flops 1572864 | bytes 9437184
  691.6 0.7 dynamic-slice_convert_fusion
  692.3 2.3 copy.14
  694.6 2.3 copy.13
  (27 shorter events, 2.0 us)
Async XLA Ops:
  7.2 106.4 %all-gather.16.cloned.1.call-start = ((), (), s32[]{:S(2)}) async-start(), calls=%async_computation.10 | async-start | bytes 4456448 | tf_op jit(solution)/shard_map/all_gather | solution.py:44
  7.9 204.8 %all-gather.14.cloned.1.call-start = ((), (), s32[]{:S(2)}) async-start(), calls=%async_computation.9 | async-start | bytes 4456448 | tf_op jit(solution)/shard_map/all_gather | solution.py:45
  8.6 252.6 %all-gather.10.cloned.1.call-start = ((), (), s32[]{:S(2)}) async-start(), calls=%async_computation.4 | async-start | bytes 5242880 | tf_op jit(solution)/shard_map/all_gather | solution.py:40
  9.4 304.7 %all-gather.12.cloned.1.call-start = ((), (), s32[]{:S(2)}) async-start(), calls=%async_computation.5 | async-start | bytes 5242880 | tf_op jit(solution)/shard_map/all_gather | solution.py:39
  10.0 357.0 %all-gather.8.cloned.1.call-start = ((), (), s32[]{:S(2)}) async-start(), calls=%async_computation.3 | async-start | bytes 5242880 | tf_op jit(solution)/shard_map/all_gather | solution.py:41
  10.5 681.7 %reduce-scatter.6.cloned.1.call-start = ((), (), s32[]{:S(2)}) async-start(), calls=%async_computation.7 | async-start | bytes 5242880 | tf_op jit(solution)/shard_map/reduce_scatter | solution.py:60
  372.3 0.6 copy-start.3
  376.2 318.4 %reduce-scatter.4.cloned.1.call-start = ((), (), s32[]{:S(2)}) async-start(), calls=%async_computation.6 | async-start | bytes 5242880 | tf_op jit(solution)/shard_map/reduce_scatter | solution.py:54
  380.4 1.9 copy-start.1
  380.4 5.1 copy-start.5
  380.4 316.4 %reduce-scatter.8.cloned.1.call-start = ((), (), s32[]{:S(2)}) async-start(), calls=%async_computation.8 | async-start | bytes 5242880 | tf_op jit(solution)/shard_map/reduce_scatter | solution.py:66
  385.5 1.3 copy-start.2
  386.8 4.4 copy-start
  386.8 4.4 copy-start.4
Sparse Core Ops, SparseCore 0:
  10.6 102.9 all-gather.15
  116.2 96.5 all-gather.13
  214.6 46.6 all-gather.9
  262.9 51.1 all-gather.11
  315.8 51.1 all-gather.7
  376.3 49.0 reduce-scatter.5
  428.2 49.0 reduce-scatter.3
  480.4 49.0 reduce-scatter.7
where the time goes:
time: 704 us
  waiting for transfers between devices  345 us (49%)
  blocking collectives  296 us (42%)
  matrix products  30.8 us (4%)
  local copies, waits for them, and re-layouts  16.2 us (2%)
  between operations  14.9 us (2%)
    unnamed x1, blocking collectives  296 us
    all_gather x1, waiting for transfers between devices, on_device(): lax.all_gather(tokens, 'row', axis=0, tiled=True)  103 us
    all_gather x1, waiting for transfers between devices, on_device(): lax.all_gather(out_grad, 'row', axis=0, tiled=True)  95.9 us
    all_gather x1, waiting for transfers between devices, on_device(): lax.all_gather(gate_weight, 'depth', axis=0, tiled=True)  49.7 us
    all_gather x1, waiting for transfers between devices, on_device(): lax.all_gather(down_weight, 'depth', axis=1, tiled=True)  49.7 us
    all_gather x1, waiting for transfers between devices, on_device(): lax.all_gather(up_weight, 'depth', axis=0, tiled=True)  43.8 us
    unnamed x17, local copies, waits for them, and re-layouts  15.5 us
  transfers between devices with their start and end apart: 8, of which 5 were waited for; matrix products, arithmetic and copies ran while one was open for 5% of the time, Pallas kernels for 0%

commit v1 on v0

--- a/solution.py
+++ b/solution.py
@@ -2,6 +2,11 @@
 import jax.numpy as jnp
 from jax import lax
 from jax.sharding import PartitionSpec as P
+
+
+def gather_from_all(value, axis, dim):
+    copies = jnp.concatenate([value] * lax.axis_size(axis), axis=dim)
+    return lax.all_to_all(copies, axis, dim, dim, tiled=True)
 
 
 def contract_rows(left, right):
@@ -38,7 +43,7 @@
     gate_full, up_full, down_full = (
         lax.all_gather(gate_weight, "depth", axis=0, tiled=True),
         lax.all_gather(up_weight, "depth", axis=0, tiled=True),
-        lax.all_gather(down_weight, "depth", axis=1, tiled=True),
+        gather_from_all(down_weight, "depth", 1),
     )
     all_tok, all_grad = (
         lax.all_gather(tokens, "row", axis=0, tiled=True),

time: 704 us -> 652 us (0.926)
  waiting for transfers between devices: 345 us -> 226 us
  blocking collectives: 296 us -> 350 us
  local copies, waits for them, and re-layouts: 16.2 us -> 31.2 us
    all_gather x1, waiting for transfers between devices: 103 us -> 33.8 us  [on_device(): lax.all_gather(tokens, 'row', axis=0, tiled=True)]
    all_to_all x0 -> x1, blocking collectives: none -> 53.7 us  [gather_from_all(): return lax.all_to_all(copies, axis, dim, dim, tiled=True)]
    all_gather x1 -> x0, waiting for transfers between devices: 49.7 us -> none  [on_device(): lax.all_gather(down_weight, 'depth', axis=1, tiled=True)]
    all_to_all x0 -> x2, local copies, waits for them, and re-layouts: none -> 12.5 us  [gather_from_all(): return lax.all_to_all(copies, axis, dim, dim, tiled=True)]
    unnamed x17 -> x22, local copies, waits for them, and re-layouts: 15.5 us -> 18.1 us
  transfers between devices with their start and end apart: 8 -> 7, of which waited for: 5 -> 4; matrix products, arithmetic and copies ran while one was open for 5% -> 8% of each run, Pallas kernels for 0% -> 0%
where the time goes in v1:
time: 652 us; the launch traced here: 651 us
  blocking collectives  350 us (54%)
  waiting for transfers between devices  226 us (35%)
  local copies, waits for them, and re-layouts  31.2 us (5%)
  matrix products  27.2 us (4%)
  between operations  14.9 us (2%)
    unnamed x1, blocking collectives  296 us
    all_gather x1, waiting for transfers between devices, on_device(): lax.all_gather(out_grad, 'row', axis=0, tiled=True)  95.9 us
    all_to_all x1, blocking collectives, gather_from_all(): return lax.all_to_all(copies, axis, dim, dim, tiled=True)  53.7 us
    all_gather x1, waiting for transfers between devices, on_device(): lax.all_gather(gate_weight, 'depth', axis=0, tiled=True)  49.7 us
    all_gather x1, waiting for transfers between devices, on_device(): lax.all_gather(up_weight, 'depth', axis=0, tiled=True)  43.8 us
    all_gather x1, waiting for transfers between devices, on_device(): lax.all_gather(tokens, 'row', axis=0, tiled=True)  33.8 us
    unnamed x22, local copies, waits for them, and re-layouts  18.1 us
  transfers between devices with their start and end apart: 7, of which 4 were waited for; matrix products, arithmetic and copies ran while one was open for 8% of the time, Pallas kernels for 0%

profile of v1, /device:TPU:2, one launch (start us, length us, event | category | flops | bytes accessed | tf_op | source)
XLA Modules:
  0.0 651.5 jit_solution(15861888783106214801)
XLA Ops:
  10.0 1.5 copy.15
  11.5 2.2 pad_maximum_fusion
  13.7 6.2 copy.19
  19.9 53.7 %all_to_all.12 = bf16[256,4,2048]{2,0,1:T(8,128)(2,1)} all-to-all(bf16[256,4,2048]{2,0,1:T(8,128)(2,1)} %copy.19), channel_id=1, replica_groups=mesh['depth'=4,'row'=16,'col'=4] {'depth'}, dimensions={1} | all-to-all | bytes 8388608 | tf_op jit(solution)/shard_map/all_to_all | solution.py:9
  73.6 6.2 copy.20
  79.8 33.8 %all-gather.13.cloned.1.call-done = bf16[16,12,8192]{2,1,0:T(8,128)(2,1)} async-done(((bf16[1,12,8192]{2,1,0:T(8,128)(2,1)}), bf16[16,12,8192]{2,1,0:T(8,128)(2,1)}) %all-gather.13.cloned.1.call-update) | async-done | bytes 3145744 | tf_op jit(solution)/shard_map/all_gather | solution.py:49
  113.6 3.2 reshape.13
  116.9 95.9 %all-gather.11.cloned.1.call-done = bf16[16,12,8192]{2,1,0:T(8,128)(2,1)} async-done(((bf16[1,12,8192]{2,1,0:T(8,128)(2,1)}), bf16[16,12,8192]{2,1,0:T(8,128)(2,1)}) %all-gather.11.cloned.1.call-update) | async-done | bytes 3145744 | tf_op jit(solution)/shard_map/all_gather | solution.py:50
  212.7 4.7 reshape.11
  217.4 43.8 %all-gather.7.cloned.1.call-done = bf16[8192,256]{1,0:T(8,128)(2,1)} async-done(((bf16[2048,256]{1,0:T(8,128)(2,1)}), bf16[8192,256]{1,0:T(8,128)(2,1)}) %all-gather.7.cloned.1.call-update) | async-done | bytes 4194320 | tf_op jit(solution)/shard_map/all_gather | solution.py:45
  261.3 3.2 fusion.5
  264.4 49.7 %all-gather.9.cloned.1.call-done = bf16[8192,256]{1,0:T(8,128)(2,1)} async-done(((bf16[2048,256]{1,0:T(8,128)(2,1)}), bf16[8192,256]{1,0:T(8,128)(2,1)}) %all-gather.9.cloned.1.call-update) | async-done | bytes 4194320 | tf_op jit(solution)/shard_map/all_gather | solution.py:44
  314.1 3.3 fusion.6
  317.5 1.1 copy-done.3
  318.5 1.6 multiply_convert_fusion.1
  320.8 3.2 fusion
  324.1 4.1 fusion.1
  328.3 1.8 copy-done.2
  330.1 3.3 convolution_convert_fusion
  334.7 4.3 fusion.7
  339.0 4.2 convolution_add_fusion
  343.2 296.2 %all-reduce.2 = bf16[192,8192]{1,0:T(8,128)(2,1)S(1)} all-reduce(f32[192,8192]{1,0:T(8,128)} %convolution_add_fusion), channel_id=2, replica_groups=mesh['depth'=4,'row'=16,'col'=4] {'row','col'}, use_global_device_ids=true, to_apply=%region_0.0.clone | all-reduce | flops 1572864 | bytes 9437184
  640.1 2.3 copy.21
  642.4 2.3 copy.22
  (33 shorter events, 4.8 us)
Async XLA Ops:
  7.2 106.4 %all-gather.13.cloned.1.call-start = ((), (), s32[]{:S(2)}) async-start(), calls=%async_computation.10 | async-start | bytes 4456448 | tf_op jit(solution)/shard_map/all_gather | solution.py:49
  7.9 204.8 %all-gather.11.cloned.1.call-start = ((), (), s32[]{:S(2)}) async-start(), calls=%async_computation.9 | async-start | bytes 4456448 | tf_op jit(solution)/shard_map/all_gather | solution.py:50
  8.6 252.6 %all-gather.7.cloned.1.call-start = ((), (), s32[]{:S(2)}) async-start(), calls=%async_computation.4 | async-start | bytes 5242880 | tf_op jit(solution)/shard_map/all_gather | solution.py:45
  9.4 304.7 %all-gather.9.cloned.1.call-start = ((), (), s32[]{:S(2)}) async-start(), calls=%async_computation.5 | async-start | bytes 5242880 | tf_op jit(solution)/shard_map/all_gather | solution.py:44
  10.0 630.2 %reduce-scatter.4.cloned.1.call-start = ((), (), s32[]{:S(2)}) async-start(), calls=%async_computation.6 | async-start | bytes 5242880 | tf_op jit(solution)/shard_map/reduce_scatter | solution.py:59
  314.1 3.3 copy-start.1
  314.1 4.4 copy-start.3
  320.2 0.6 copy-start.4
  324.1 318.3 %reduce-scatter.6.cloned.1.call-start = ((), (), s32[]{:S(2)}) async-start(), calls=%async_computation.7 | async-start | bytes 5242880 | tf_op jit(solution)/shard_map/reduce_scatter | solution.py:65
  328.2 1.9 copy-start.2
  328.2 5.2 copy-start.7
  328.3 316.4 %reduce-scatter.8.cloned.1.call-start = ((), (), s32[]{:S(2)}) async-start(), calls=%async_computation.8 | async-start | bytes 5242880 | tf_op jit(solution)/shard_map/reduce_scatter | solution.py:71
  333.4 1.3 copy-start.5
  334.7 4.3 copy-start
  334.7 4.3 copy-start.6
Sparse Core Ops, SparseCore 0:
  10.6 102.9 all-gather.12
  116.2 96.5 all-gather.10
  214.6 46.6 all-gather.6
  262.9 51.1 all-gather.8
  324.2 49.0 reduce-scatter.3
  375.9 49.1 reduce-scatter.5
  428.2 49.0 reduce-scatter.7
